TPU v7x, 256 devices: a whole 4x4x8 slice. The times are simulated.
256 devices in a mesh: row: 16 (over z_hi, y, core), col: 16 (over z_lo, x).
Axes of the slice: x: 4, y: 4, z: 8 (z_hi: 2, z_lo: 4; z = z_hi * 4 + z_lo), core: 2. Of those that a mesh axis runs over, the one named last changes fastest.
Arguments:
- features: bfloat16 [65536, 128], P(('col', 'row')), may hold values from -6 to 6
- weight: bfloat16 [128, 128], replicated, may hold values from -0.5 to 0.5
- tiles: bfloat16 [16, 16, 352, 128, 128], P('row', 'col'), may hold values from -0.0546875 to 0.0546875
- tile_slots: int32 [16, 16, 352], P('row', 'col'), may hold values from 0 to 1023, as said below
- tile_counts: int32 [16, 16], P('row', 'col'), may hold values from 44 to 352, as said below
- cotangent: bfloat16 [65536, 128], P(('row', 'col')), may hold values from -6 to 6
Outputs:
- hidden: bfloat16 [65536, 128], P(('row', 'col'))
- feature_grad: bfloat16 [65536, 128], P(('col', 'row'))
- weight_grad: float32 [128, 128], replicated
Inputs may be any that keep to these rules, and one draw needn't show every extreme that they name: `tile_slots`: the slots of one block are distinct. `tile_counts`: some block has all 352 slots live.
All inputs are finite; a program needn't handle non-finite values.
Results may differ from a plain program's by a relative error of at most 0.006.
Values may be sent and summed in bfloat16 or wider, within the bound.
A program may use at most 128 MiB of HBM per device.

v0:
```python
import math
import jax
import jax.numpy as jnp
from jax import lax
from jax.sharding import PartitionSpec as P


def silu_grad(values):
    sig = jax.nn.sigmoid(values)
    return sig * (1.0 + values * (1.0 - sig))


def body(features, weight, tiles, tile_slots, tile_counts, cotangent):
    tile_vals = tiles[0, 0]
    slot_ids = tile_slots[0, 0]
    live_count = tile_counts[0, 0]
    tile_size = tile_vals.shape[-1]
    share_rows = features.shape[0]
    width = features.shape[1]
    slot_total = slot_ids.shape[0]
    row_count = lax.axis_size("row")
    col_count = lax.axis_size("col")
    tile_rows = share_rows * col_count // tile_size
    tile_cols = share_rows * row_count // tile_size
    col_index = lax.axis_index("col")
    projected = jnp.dot(features, weight, preferred_element_type=jnp.float32).astype(jnp.bfloat16)
    proj_block = lax.all_gather(projected, "row", axis=0, tiled=True)
    is_live = jnp.arange(slot_total, dtype=jnp.int32) < live_count
    gathered = proj_block.reshape(tile_cols, tile_size, width)[slot_ids % tile_cols]
    products = jnp.einsum("tij,tjf->tif", tile_vals, gathered, preferred_element_type=jnp.float32)
    fwd_targets = jnp.where(is_live, slot_ids // tile_cols, tile_rows)
    partial_value = jax.ops.segment_sum(products, fwd_targets, tile_rows + 1)[:tile_rows].reshape(
        tile_rows * tile_size, width
    )
    summed = lax.psum(partial_value, "col")
    own_rows = lax.dynamic_slice_in_dim(summed, col_index * share_rows, share_rows, 0)
    hidden = jax.nn.silu(own_rows).astype(jnp.bfloat16)
    cot_block = lax.all_gather(cotangent, "col", axis=0, tiled=True)
    grad_block = (cot_block.astype(jnp.float32) * silu_grad(summed)).astype(jnp.bfloat16)
    grad_tiles = grad_block.reshape(tile_rows, tile_size, width)[slot_ids // tile_cols]
    back_products = jnp.einsum(
        "tji,tjf->tif", tile_vals, grad_tiles, preferred_element_type=jnp.float32
    )
    back_targets = jnp.where(is_live, slot_ids % tile_cols, tile_cols)
    back_partial = jax.ops.segment_sum(back_products, back_targets, tile_cols + 1)[
        :tile_cols
    ].reshape(tile_cols * tile_size, width)
    grad_proj = lax.psum_scatter(back_partial, "row", scatter_dimension=0, tiled=True).astype(
        jnp.bfloat16
    )
    feature_grad = jnp.dot(grad_proj, weight.T, preferred_element_type=jnp.float32).astype(
        jnp.bfloat16
    )
    weight_term = jnp.dot(features.T, grad_proj, preferred_element_type=jnp.float32)
    node_total = share_rows * row_count * col_count
    weight_grad = lax.psum(weight_term, ("row", "col")) / math.sqrt(node_total)
    return (hidden, feature_grad, weight_grad)


def solution(mesh):
    placed = (
        P(("col", "row"), None),
        P(),
        P("row", "col", None, None, None),
        P("row", "col", None),
        P("row", "col"),
        P(("row", "col"), None),
    )
    return jax.shard_map(
        body,
        mesh=mesh,
        in_specs=placed,
        out_specs=(P(("row", "col"), None), P(("col", "row"), None), P()),
        check_vma=False,
    )
```

profile of v0, /device:TPU:1, one launch (start us, length us, event | category | flops | bytes accessed | tf_op | source)
XLA Modules:
  0.0 771.6 jit_solution(9133756063964806921)
XLA Ops:
  7.2 0.8 copy-done
  8.0 1.5 convolution_convert_fusion.1
  11.0 0.7 fusion.15
  11.7 0.7 fusion.13
  12.4 58.8 %all-gather.3.cloned.1.call-done = bf16[4096,128]{1,0:T(8,128)(2,1)} async-done(((bf16[256,128]{1,0:T(8,128)(2,1)}), bf16[4096,128]{1,0:T(8,128)(2,1)}) %all-gather.3.cloned.1.call-update) | async-done | bytes 1048592 | tf_op jit(solution)/shard_map/all_gather | solution.py:27
  71.3 12.2 %gather_fusion = bf16[352,128,128]{2,1,0:T(8,128)(2,1)} fusion(bf16[32,128,128]{2,1,0:T(8,128)(2,1)} %bitcast.41, s32[1024]{0:T(1024)S(1)} %pad_clamp_fusion.1), kind=kCustom, calls=%fused_computation | custom fusion | bytes 23070080 | tf_op jit(solution)/shard_map/gather | solution.py:29
  83.5 20.6 %fusion.4 = f32[352,128,128]{1,2,0:T(8,128)} fusion(bf16[352,128,128]{2,1,0:T(8,128)(2,1)} %gather_fusion, bf16[1,1,352,128,128]{4,3,2,1,0:T(8,128)(2,1)} %param.8), kind=kOutput, calls=%fused_computation.8 | convolution fusion | flops 1476395008 | bytes 46137344 | tf_op jit(solution)/shard_map/tij,tjf->tif/dot_general | solution.py:30
  104.1 23.5 %copy.13 = f32[352,128,128]{2,1,0:T(8,128)} copy(f32[352,128,128]{1,2,0:T(8,128)} %fusion.4) | data formatting | bytes 46137344 | tf_op jit(solution)/shard_map/tij,tjf->tif/dot_general | solution.py:30
  127.8 46.0 %scatter_fusion = f32[33,128,128]{2,1,0:T(8,128)S(1)} fusion(f32[33,128,128]{2,1,0:T(8,128)S(1)} %broadcast.191.clone, s32[352]{0:T(512)S(1)} %get-tuple-element.10, f32[352,128,128]{2,1,0:T(8,128)} %copy.13), kind=kCustom, calls=%fused_computation.2 | custom fusion | flops 5767168 | bytes 69207424 | tf_op jit(solution)/shard_map/scatter-add | solution.py:32
  173.9 1.5 slice.12
  175.7 153.0 %all-reduce.3.cloned.1.call-done = f32[4096,128]{1,0:T(8,128)} async-done(((f32[4096,128]{1,0:T(8,128)}), f32[4096,128]{1,0:T(8,128)}) %all-reduce.3.cloned.1.call-update) | async-done | bytes 2097168 | tf_op jit(solution)/shard_map/psum | solution.py:35
  328.6 2.6 multiply_convert_fusion
  331.3 11.0 %gather_fusion.1 = bf16[352,128,128]{2,1,0:T(8,128)(2,1)} fusion(bf16[32,128,128]{2,1,0:T(8,128)(2,1)S(1)} %bitcast.40, s32[1024]{0:T(1024)S(1)} %pad_clamp_fusion), kind=kCustom, calls=%fused_computation.1 | custom fusion | bytes 23070080 | tf_op jit(solution)/shard_map/gather | solution.py:40
  342.3 14.4 %fusion.7 = f32[352,128,128]{1,2,0:T(8,128)} fusion(bf16[352,128,128]{2,1,0:T(8,128)(2,1)} %gather_fusion.1, bf16[1,1,352,128,128]{4,3,2,1,0:T(8,128)(2,1)} %param.8), kind=kOutput, calls=%fused_computation.9 | convolution fusion | flops 1476395008 | bytes 46137344 | tf_op jit(solution)/shard_map/tji,tjf->tif/dot_general | solution.py:41
  356.7 23.5 %copy.15 = f32[352,128,128]{2,1,0:T(8,128)} copy(f32[352,128,128]{1,2,0:T(8,128)} %fusion.7) | data formatting | bytes 46137344 | tf_op jit(solution)/shard_map/tji,tjf->tif/dot_general | solution.py:41
  380.4 46.0 %scatter_fusion.1 = f32[33,128,128]{2,1,0:T(8,128)S(1)} fusion(f32[33,128,128]{2,1,0:T(8,128)S(1)} %broadcast.191, s32[352]{0:T(512)S(1)} %get-tuple-element.11, f32[352,128,128]{2,1,0:T(8,128)} %copy.15), kind=kCustom, calls=%fused_computation.3 | custom fusion | flops 5767168 | bytes 69207424 | tf_op jit(solution)/shard_map/scatter-add | solution.py:45
  426.4 1.5 slice.13
  428.0 1.6 multiply_convert_fusion.1
  429.6 92.6 %reduce-scatter.2.cloned.1.call-done = f32[256,128]{1,0:T(8,128)} async-done(((f32[4096,128]{1,0:T(8,128)}), f32[256,128]{1,0:T(8,128)}) %reduce-scatter.2.cloned.1.call-update) | async-done | bytes 131088 | tf_op jit(solution)/shard_map/reduce_scatter | solution.py:48
  522.2 1.7 convolution_bitcast_fusion
  524.0 1.7 convolution_convert_fusion
  525.7 237.9 %all-reduce.5.cloned.1.call-done = f32[128,128]{0,1:T(8,128)} async-done(((f32[128,128]{0,1:T(8,128)}), f32[128,128]{0,1:T(8,128)}) %all-reduce.5.cloned.1.call-update) | async-done | bytes 65552 | tf_op jit(solution)/shard_map/psum | solution.py:56
  763.5 0.8 broadcast_multiply_fusion
  764.4 0.7 copy.16
  (18 shorter events, 1.7 us)
Async XLA Ops:
  7.2 0.8 copy-start
  7.2 64.1 %all-gather.3.cloned.1.call-start = ((), (), s32[]{:S(2)}) async-start(), calls=%async_computation.1 | async-start | bytes 1114112 | tf_op jit(solution)/shard_map/all_gather | solution.py:27
  9.6 166.1 %all-gather.5.cloned.1.call-start = ((), (), s32[]{:S(2)}) async-start(), calls=%async_computation.3 | async-start | bytes 1114112 | tf_op jit(solution)/shard_map/all_gather | solution.py:38
  10.3 318.3 %all-reduce.3.cloned.1.call-start = ((), (), s32[]{:S(2)}) async-start(), calls=%async_computation.2 | async-start | bytes 4194304 | tf_op jit(solution)/shard_map/psum | solution.py:35
  175.4 346.8 %reduce-scatter.2.cloned.1.call-start = ((), (), s32[]{:S(2)}) async-start(), calls=%async_computation.4 | async-start | bytes 2228224 | tf_op jit(solution)/shard_map/reduce_scatter | solution.py:48
  380.4 143.5 %copy-start.1 = (bf16[128,128]{1,0:T(8,128)(2,1)S(1)}, bf16[128,128]{1,0:T(8,128)(2,1)}, u32[]{:S(2)}) copy-start(bf16[128,128]{1,0:T(8,128)(2,1)} %param.7) | copy-start | bytes 98308
  428.0 335.5 %all-reduce.5.cloned.1.call-start = ((), (), s32[]{:S(2)}) async-start(), calls=%async_computation.5 | async-start | bytes 131072 | tf_op jit(solution)/shard_map/psum | solution.py:56
Sparse Core Ops, SparseCore 0:
  11.3 59.9 all-gather.2
  73.1 65.9 all-gather.4
  175.5 153.0 all-reduce.2
  428.1 94.0 reduce-scatter.1
  528.1 235.3 all-reduce.4
where the time goes:
time: 774 us; the launch traced here: 772 us
  waiting for transfers between devices  543 us (70%)
  other arithmetic  98.5 us (13%)
  local copies, waits for them, and re-layouts  75.1 us (10%)
  matrix products  40 us (5%)
  between operations  14.5 us (2%)
    psum x1, waiting for transfers between devices, body(): weight_grad = lax.psum(weight_term, ('row', 'col')) / math.sqrt(node_total)  238 us
    psum x1, waiting for transfers between devices, body(): summed = lax.psum(partial_value, 'col')  153 us
    reduce_scatter x1, waiting for transfers between devices, body(): lax.psum_scatter(back_partial, 'row', scatter_dimension=0, tiled=True)  92.6 us
    all_gather x1, waiting for transfers between devices, body(): proj_block = lax.all_gather(projected, 'row', axis=0, tiled=True)  58.8 us
    scatter-add x1, other arithmetic, body(): jax.ops.segment_sum(products, fwd_targets, tile_rows + 1)[:tile_rows]  46 us
    scatter-add x1, other arithmetic, body(): jax.ops.segment_sum(back_products, back_targets, tile_cols + 1)[:tile_cols]  46 us
    dot_general x1, local copies, waits for them, and re-layouts, body(): jnp.einsum('tij,tjf->tif', tile_vals, gathered, preferred_element_type=jn...  23.5 us
    dot_general x1, local copies, waits for them, and re-layouts, body(): jnp.einsum('tji,tjf->tif', tile_vals, grad_tiles, preferred_element_type=...  23.5 us
  transfers between devices with their start and end apart: 5, of which 4 were waited for; matrix products, arithmetic and copies ran while one was open for 14% of the time, Pallas kernels for 0%

commit v1 on v0

--- a/solution.py
+++ b/solution.py
@@ -32,7 +32,8 @@
     partial_value = jax.ops.segment_sum(products, fwd_targets, tile_rows + 1)[:tile_rows].reshape(
         tile_rows * tile_size, width
     )
-    summed = lax.psum(partial_value, "col")
+    parts = lax.all_gather(partial_value, "col", axis=0, tiled=False)
+    summed = parts.sum(axis=0)
     own_rows = lax.dynamic_slice_in_dim(summed, col_index * share_rows, share_rows, 0)
     hidden = jax.nn.silu(own_rows).astype(jnp.bfloat16)
     cot_block = lax.all_gather(cotangent, "col", axis=0, tiled=True)

time: 774 us -> 1040 us (1.34)
  waiting for transfers between devices: 543 us -> 799 us
  other arithmetic: 98.5 us -> 110 us
    all_gather x0 -> x1, waiting for transfers between devices: none -> 350 us  [body(): parts = lax.all_gather(partial_value, 'col', axis=0, tiled=False)]
    psum x1 -> x0, waiting for transfers between devices: 153 us -> none  [body(): summed = lax.psum(partial_value, 'col')]
    all_gather x1, waiting for transfers between devices: 0.02 us -> 57.6 us  [body(): cot_block = lax.all_gather(cotangent, 'col', axis=0, tiled=True)]
    reduce_sum x0 -> x1, other arithmetic: none -> 11.8 us  [body(): summed = parts.sum(axis=0)]
  transfers between devices with their start and end apart: 5 -> 5, of which waited for: 4 -> 5; matrix products, arithmetic and copies ran while one was open for 14% -> 2% of each run, Pallas kernels for 0% -> 0%
where the time goes in v1:
time: 1040 us
  waiting for transfers between devices  799 us (77%)
  other arithmetic  110 us (11%)
  local copies, waits for them, and re-layouts  75.1 us (7%)
  matrix products  40 us (4%)
  between operations  14.5 us (1%)
    all_gather x1, waiting for transfers between devices, body(): parts = lax.all_gather(partial_value, 'col', axis=0, tiled=False)  350 us
    psum x1, waiting for transfers between devices, body(): weight_grad = lax.psum(weight_term, ('row', 'col')) / math.sqrt(node_total)  238 us
    reduce_scatter x1, waiting for transfers between devices, body(): lax.psum_scatter(back_partial, 'row', scatter_dimension=0, tiled=True)  93.2 us
    all_gather x1, waiting for transfers between devices, body(): proj_block = lax.all_gather(projected, 'row', axis=0, tiled=True)  59.6 us
    all_gather x1, waiting for transfers between devices, body(): cot_block = lax.all_gather(cotangent, 'col', axis=0, tiled=True)  57.6 us
    scatter-add x1, other arithmetic, body(): jax.ops.segment_sum(products, fwd_targets, tile_rows + 1)[:tile_rows]  46 us
    scatter-add x1, other arithmetic, body(): jax.ops.segment_sum(back_products, back_targets, tile_cols + 1)[:tile_cols]  46 us
    dot_general x1, local copies, waits for them, and re-layouts, body(): jnp.einsum('tji,tjf->tif', tile_vals, grad_tiles, preferred_element_type=...  23.5 us
  transfers between devices with their start and end apart: 5, of which 5 were waited for; matrix products, arithmetic and copies ran while one was open for 2% of the time, Pallas kernels for 0%

profile of v1, /device:TPU:1, one launch (start us, length us, event | category | flops | bytes accessed | tf_op | source)
XLA Modules:
  0.0 1038.2 jit_solution(16585602846013943177)
XLA Ops:
  7.2 0.8 copy-done
  8.0 1.5 convolution_convert_fusion.1
  11.7 59.6 %all-gather.4.cloned.1.call-done = bf16[4096,128]{1,0:T(8,128)(2,1)} async-done(((bf16[256,128]{1,0:T(8,128)(2,1)}), bf16[4096,128]{1,0:T(8,128)(2,1)}) %all-gather.4.cloned.1.call-update) | async-done | bytes 1048592 | tf_op jit(solution)/shard_map/all_gather | solution.py:27
  71.3 12.2 %gather_fusion = bf16[352,128,128]{2,1,0:T(8,128)(2,1)} fusion(bf16[32,128,128]{2,1,0:T(8,128)(2,1)} %bitcast.41, s32[1024]{0:T(1024)S(1)} %pad_clamp_fusion.1), kind=kCustom, calls=%fused_computation | custom fusion | bytes 23070080 | tf_op jit(solution)/shard_map/gather | solution.py:29
  83.5 20.6 %fusion.4 = f32[352,128,128]{1,2,0:T(8,128)} fusion(bf16[352,128,128]{2,1,0:T(8,128)(2,1)} %gather_fusion, bf16[1,1,352,128,128]{4,3,2,1,0:T(8,128)(2,1)} %param.8), kind=kOutput, calls=%fused_computation.8 | convolution fusion | flops 1476395008 | bytes 46137344 | tf_op jit(solution)/shard_map/tij,tjf->tif/dot_general | solution.py:30
  104.1 23.5 %copy.18 = f32[352,128,128]{2,1,0:T(8,128)} copy(f32[352,128,128]{1,2,0:T(8,128)} %fusion.4) | data formatting | bytes 46137344 | tf_op jit(solution)/shard_map/tij,tjf->tif/dot_general | solution.py:30
  127.8 46.0 %scatter_fusion = f32[33,128,128]{2,1,0:T(8,128)S(1)} fusion(f32[33,128,128]{2,1,0:T(8,128)S(1)} %broadcast.191.clone, s32[352]{0:T(512)S(1)} %get-tuple-element.13, f32[352,128,128]{2,1,0:T(8,128)} %copy.18), kind=kCustom, calls=%fused_computation.2 | custom fusion | flops 5767168 | bytes 69207424 | tf_op jit(solution)/shard_map/scatter-add | solution.py:32
  173.8 1.5 slice.12
  176.3 349.5 %all-gather.6.cloned.1.call-done = f32[16,4096,128]{2,1,0:T(8,128)} async-done(((f32[1,4096,128]{2,1,0:T(8,128)}), f32[16,4096,128]{2,1,0:T(8,128)}) %all-gather.6.cloned.1.call-update) | async-done | bytes 33554448 | tf_op jit(solution)/shard_map/all_gather | solution.py:35
  525.8 11.8 %reduce_sum.9 = f32[4096,128]{1,0:T(8,128)S(1)} reduce(f32[16,4096,128]{2,1,0:T(8,128)} %all-gather.6.cloned.1.call-done, f32[]{:T(128)} %constant.42.clone.1), dimensions={0}, to_apply=%region_1.2 | reduce | flops 7864320 | bytes 35651588 | tf_op jit(solution)/shard_map/reduce_sum | solution.py:36
  537.6 57.6 %all-gather.8.cloned.1.call-done = bf16[4096,128]{1,0:T(8,128)(2,1)} async-done(((bf16[256,128]{1,0:T(8,128)(2,1)}), bf16[4096,128]{1,0:T(8,128)(2,1)}) %all-gather.8.cloned.1.call-update) | async-done | bytes 1048592 | tf_op jit(solution)/shard_map/all_gather | solution.py:39
  595.2 2.0 multiply_convert_fusion
  597.2 11.0 %gather_fusion.1 = bf16[352,128,128]{2,1,0:T(8,128)(2,1)} fusion(bf16[32,128,128]{2,1,0:T(8,128)(2,1)S(1)} %bitcast.40, s32[1024]{0:T(1024)S(1)} %pad_clamp_fusion), kind=kCustom, calls=%fused_computation.1 | custom fusion | bytes 23070080 | tf_op jit(solution)/shard_map/gather | solution.py:41
  608.2 14.4 %fusion.7 = f32[352,128,128]{1,2,0:T(8,128)} fusion(bf16[352,128,128]{2,1,0:T(8,128)(2,1)} %gather_fusion.1, bf16[1,1,352,128,128]{4,3,2,1,0:T(8,128)(2,1)} %param.8), kind=kOutput, calls=%fused_computation.9 | convolution fusion | flops 1476395008 | bytes 46137344 | tf_op jit(solution)/shard_map/tji,tjf->tif/dot_general | solution.py:42
  622.6 23.5 %copy.20 = f32[352,128,128]{2,1,0:T(8,128)} copy(f32[352,128,128]{1,2,0:T(8,128)} %fusion.7) | data formatting | bytes 46137344 | tf_op jit(solution)/shard_map/tji,tjf->tif/dot_general | solution.py:42
  646.3 46.0 %scatter_fusion.1 = f32[33,128,128]{2,1,0:T(8,128)S(1)} fusion(f32[33,128,128]{2,1,0:T(8,128)S(1)} %broadcast.191, s32[352]{0:T(512)S(1)} %get-tuple-element.14, f32[352,128,128]{2,1,0:T(8,128)} %copy.20), kind=kCustom, calls=%fused_computation.3 | custom fusion | flops 5767168 | bytes 69207424 | tf_op jit(solution)/shard_map/scatter-add | solution.py:46
  692.3 1.5 slice.13
  693.9 1.6 multiply_convert_fusion.1
  695.5 93.2 %reduce-scatter.2.cloned.1.call-done = f32[256,128]{1,0:T(8,128)} async-done(((f32[4096,128]{1,0:T(8,128)}), f32[256,128]{1,0:T(8,128)}) %reduce-scatter.2.cloned.1.call-update) | async-done | bytes 131088 | tf_op jit(solution)/shard_map/reduce_scatter | solution.py:49
  788.7 1.7 convolution_bitcast_fusion
  790.5 1.7 convolution_convert_fusion
  792.2 238.0 %all-reduce.2.cloned.1.call-done = f32[128,128]{0,1:T(8,128)} async-done(((f32[128,128]{0,1:T(8,128)}), f32[128,128]{0,1:T(8,128)}) %all-reduce.2.cloned.1.call-update) | async-done | bytes 65552 | tf_op jit(solution)/shard_map/psum | solution.py:57
  1030.1 0.8 broadcast_multiply_fusion
  1031.0 0.7 copy.21
  (21 shorter events, 3.1 us)
Async XLA Ops:
  7.2 0.8 copy-start
  7.2 64.1 %all-gather.4.cloned.1.call-start = ((), (), s32[]{:S(2)}) async-start(), calls=%async_computation.1 | async-start | bytes 1114112 | tf_op jit(solution)/shard_map/all_gather | solution.py:27
  9.6 516.2 %all-gather.6.cloned.1.call-start = ((), (), s32[]{:S(2)}) async-start(), calls=%async_computation.2 | async-start | bytes 35651584 | tf_op jit(solution)/shard_map/all_gather | solution.py:35
  175.3 419.9 %all-gather.8.cloned.1.call-start = ((), (), s32[]{:S(2)}) async-start(), calls=%async_computation.3 | async-start | bytes 1114112 | tf_op jit(solution)/shard_map/all_gather | solution.py:39
  176.0 612.7 %reduce-scatter.2.cloned.1.call-start = ((), (), s32[]{:S(2)}) async-start(), calls=%async_computation.4 | async-start | bytes 2228224 | tf_op jit(solution)/shard_map/reduce_scatter | solution.py:49
  537.6 70.6 %copy-start.1 = (f32[4096,128]{1,0:T(8,128)}, f32[4096,128]{1,0:T(8,128)S(1)}, u32[]{:S(2)}) copy-start(f32[4096,128]{1,0:T(8,128)S(1)} %reduce_sum.9) | copy-start | bytes 6291460
  646.3 144.1 %copy-start.2 = (bf16[128,128]{1,0:T(8,128)(2,1)S(1)}, bf16[128,128]{1,0:T(8,128)(2,1)}, u32[]{:S(2)}) copy-start(bf16[128,128]{1,0:T(8,128)(2,1)} %param.7) | copy-start | bytes 98308
  693.9 336.3 %all-reduce.2.cloned.1.call-start = ((), (), s32[]{:S(2)}) async-start(), calls=%async_computation.5 | async-start | bytes 131072 | tf_op jit(solution)/shard_map/psum | solution.py:57
Sparse Core Ops, SparseCore 0:
  11.3 59.9 all-gather.3
  175.4 350.3 all-gather.5
  527.6 67.5 all-gather.7
  694.0 94.6 reduce-scatter.1
  794.6 235.4 all-reduce.1
